TPU v7x, 32 devices: a whole 2x2x4 slice. The times are simulated.
32 devices in a mesh: space: 2 (over y), tensor: 16 (over z, x, core).
Axes of the slice: x: 2, y: 2, z: 4, core: 2. Of those that a mesh axis runs over, the one named last changes fastest.
Arguments:
- tokens: bfloat16 [784, 6144], P('space', 'tensor'), may hold values from -6 to 6
- grad_out: bfloat16 [784, 6144], P('space', 'tensor'), may hold values from -6 to 6
- w_in: bfloat16 [6144, 12288], P(None, 'tensor'), may hold values from -0.078125 to 0.078125
- w_out: bfloat16 [12288, 6144], P('tensor'), may hold values from -0.0546875 to 0.0546875
- conv_kernel: float32 [9, 12288], P(None, 'tensor'), may hold values from -2 to 2
- conv_bias: float32 [12288], P('tensor'), may hold values from -3 to 3
Outputs:
- grad_tokens: bfloat16 [784, 6144], P('space', 'tensor')
- grad_w_in: bfloat16 [6144, 12288], P('space', 'tensor')
- grad_w_out: bfloat16 [12288, 6144], P('tensor', 'space')
- grad_kernel: float32 [9, 12288], P(None, 'tensor')
- grad_bias: float32 [12288], P('tensor')
All inputs are finite; a program needn't handle non-finite values.
Results may differ from a plain program's by a relative error of at most 0.014.
Values may be sent and summed in bfloat16 or wider, within the bound.
No kernel may reach another device: no remote copies, remote signals or barrier semaphores. Data moves between devices by JAX's collectives and lax.ppermute only.
A program may use at most 192 MiB of HBM per device.

v0:
```python
import jax
import jax.numpy as jnp
from jax import lax
from jax.sharding import PartitionSpec as P

GW = 56
OFFSETS = [(-1, -1), (-1, 0), (-1, 1), (0, -1), (0, 0), (0, 1), (1, -1), (1, 0), (1, 1)]


def padded_2(block, sides, width):
    for axis, dim in sides:
        count = lax.axis_size(axis)
        forward = [(i, i + 1) for i in range(count - 1)]
        backward = [(target, source) for source, target in forward]
        low = lax.ppermute(
            lax.slice_in_dim(block, block.shape[dim] - width, None, axis=dim), axis, forward
        )
        high = lax.ppermute(lax.slice_in_dim(block, 0, width, axis=dim), axis, backward)
        block = jnp.concatenate([low, block, high], axis=dim)
    return block


def gelu_parts(pre):
    inner = 0.7978845608 * (pre + 0.044715 * pre * pre * pre)
    tanh_val = jnp.tanh(inner)
    value = 0.5 * pre * (1.0 + tanh_val)
    slope = 0.5 * (1.0 + tanh_val) + 0.5 * pre * (1.0 - tanh_val * tanh_val) * 0.7978845608 * (
        1.0 + 3.0 * 0.044715 * pre * pre
    )
    return (value, slope)


def shards(tokens, grad_out, w_in, w_out, conv_kernel, conv_bias):
    tok_rows = tokens.shape[0]
    grid_rows = tok_rows // GW
    ff_local = w_in.shape[1]
    full_tokens, full_grad = (
        lax.all_gather(tokens, "tensor", axis=1, tiled=True),
        lax.all_gather(grad_out, "tensor", axis=1, tiled=True),
    )
    hidden_acc = jnp.dot(full_tokens, w_in, preferred_element_type=jnp.float32)
    grad_act = lax.dot_general(
        full_grad, w_out, (((1,), (1,)), ((), ())), preferred_element_type=jnp.float32
    )
    hidden = hidden_acc.astype(jnp.bfloat16).reshape(grid_rows, GW, ff_local)
    rimmed = padded_2(hidden, (("space", 0),), 1)
    padded = jnp.pad(rimmed, ((0, 0), (1, 1), (0, 0))).astype(jnp.float32)
    pre = jnp.zeros((grid_rows, GW, ff_local), jnp.float32) + conv_bias
    for index, (da, db) in enumerate(OFFSETS):
        pre = pre + conv_kernel[index] * padded[1 + da : 1 + da + grid_rows, 1 + db : 1 + db + GW]
    act, slope = gelu_parts(pre)
    act = act.astype(jnp.bfloat16).reshape(tok_rows, ff_local)
    grad_pre = (grad_act.reshape(grid_rows, GW, ff_local) * slope).astype(jnp.bfloat16)
    out_term = lax.dot_general(
        act, full_grad, (((0,), (0,)), ((), ())), preferred_element_type=jnp.float32
    )
    grad_f = grad_pre.astype(jnp.float32)
    kernel_rows = []
    for index, (da, db) in enumerate(OFFSETS):
        kernel_rows.append(
            jnp.sum(grad_f * padded[1 + da : 1 + da + grid_rows, 1 + db : 1 + db + GW], axis=(0, 1))
        )
    kernel_terms = jnp.stack(kernel_rows)
    bias_term = jnp.sum(grad_f, axis=(0, 1))
    grad_kernel, grad_bias = lax.psum((kernel_terms, bias_term), "space")
    grad_rimmed = padded_2(grad_pre, (("space", 0),), 1)
    grad_padded = jnp.pad(grad_rimmed, ((0, 0), (1, 1), (0, 0))).astype(jnp.float32)
    grad_hidden = jnp.zeros((grid_rows, GW, ff_local), jnp.float32)
    for index, (da, db) in enumerate(OFFSETS):
        grad_hidden = (
            grad_hidden
            + conv_kernel[index] * grad_padded[1 - da : 1 - da + grid_rows, 1 - db : 1 - db + GW]
        )
    grad_hidden = grad_hidden.astype(jnp.bfloat16).reshape(tok_rows, ff_local)
    in_term = lax.dot_general(
        full_tokens, grad_hidden, (((0,), (0,)), ((), ())), preferred_element_type=jnp.float32
    )
    summed_in, summed_out = (
        lax.psum_scatter(
            in_term.astype(jnp.bfloat16), "space", scatter_dimension=0, tiled=True
        ).astype(jnp.float32),
        lax.psum_scatter(
            out_term.astype(jnp.bfloat16), "space", scatter_dimension=1, tiled=True
        ).astype(jnp.float32),
    )
    grad_w_in = summed_in.astype(jnp.bfloat16)
    grad_w_out = summed_out.astype(jnp.bfloat16)
    token_terms = lax.dot_general(
        grad_hidden, w_in, (((1,), (1,)), ((), ())), preferred_element_type=jnp.float32
    )
    grad_tokens = lax.psum_scatter(
        token_terms.astype(jnp.bfloat16), "tensor", scatter_dimension=1, tiled=True
    )
    return (grad_tokens, grad_w_in, grad_w_out, grad_kernel, grad_bias)


def solution(mesh):
    return jax.shard_map(
        shards,
        mesh=mesh,
        in_specs=(
            P("space", "tensor"),
            P("space", "tensor"),
            P(None, "tensor"),
            P("tensor", None),
            P(None, "tensor"),
            P("tensor"),
        ),
        out_specs=(
            P("space", "tensor"),
            P("space", "tensor"),
            P("tensor", "space"),
            P(None, "tensor"),
            P("tensor"),
        ),
        check_vma=False,
    )
```

profile of v0, /device:TPU:0, one launch (start us, length us, event | category | flops | bytes accessed | tf_op | source)
XLA Modules:
  0.0 478.0 jit_solution(18130688776964309026)
XLA Ops:
  7.2 0.7 all-gather.5.cloned.1.call-update
  7.9 0.7 all-gather.3.cloned.1.call-update
  8.7 1.1 slice_reduce_fusion.8
  9.8 59.7 %all-gather.5.cloned.1.call-done = bf16[392,6144]{1,0:T(8,128)(2,1)} async-done(((bf16[392,384]{1,0:T(8,128)(2,1)}), bf16[392,6144]{1,0:T(8,128)(2,1)}) %all-gather.5.cloned.1.call-update) | async-done | bytes 4816912 | tf_op jit(solution)/shard_map/all_gather | solution.py:38
  69.5 9.0 %convolution_convert_fusion.3 = bf16[392,768]{1,0:T(8,128)(2,1)S(1)} fusion(bf16[392,6144]{1,0:T(8,128)(2,1)} %all-gather.5.cloned.1.call-done, bf16[6144,768]{1,0:T(8,128)(2,1)} %param.8), kind=kOutput, calls=%fused_computation.19 | convolution fusion | flops 3699677184 | bytes 14856192 | tf_op jit(solution)/shard_map/dot_general | solution.py:41
  78.6 3.4 collective-permute-start
  82.0 1.3 collective-permute-start.1
  83.3 43.2 %all-gather.3.cloned.1.call-done = bf16[392,6144]{1,0:T(8,128)(2,1)} async-done(((bf16[392,384]{1,0:T(8,128)(2,1)}), bf16[392,6144]{1,0:T(8,128)(2,1)}) %all-gather.3.cloned.1.call-update) | async-done | bytes 4816912 | tf_op jit(solution)/shard_map/all_gather | solution.py:39
  126.5 8.2 %fusion.36 = f32[392,768]{1,0:T(8,128)S(1)} fusion(bf16[392,6144]{1,0:T(8,128)(2,1)} %all-gather.3.cloned.1.call-done, bf16[768,6144]{1,0:T(8,128)(2,1)} %param.9), kind=kOutput, calls=%fused_computation.77 | convolution fusion | flops 3699376128 | bytes 15458304 | tf_op jit(solution)/shard_map/dot_general | solution.py:42
  134.8 0.2 fusion.33
  135.0 0.4 copy-done
  135.5 3.1 fusion.17
  138.6 3.4 collective-permute-start.2
  142.0 1.3 collective-permute-start.3
  143.3 0.9 collective-permute-done.2
  144.1 4.2 collective-permute-done.3
  148.3 0.2 fusion.27
  148.6 0.9 fusion.19
  149.5 0.3 slice-done.2
  149.8 5.6 %convolution_convert_fusion.2 = bf16[392,6144]{1,0:T(8,128)(2,1)} fusion(bf16[392,768]{1,0:T(8,128)(2,1)S(1)} %bitcast.25, bf16[6144,768]{1,0:T(8,128)(2,1)S(1)} %bitcast.30), kind=kOutput, calls=%fused_computation.3 | convolution fusion | flops 3701784576 | bytes 14856192 | tf_op jit(solution)/shard_map/dot_general | solution.py:88
  155.4 8.0 %copy.13 = bf16[392,6144]{0,1:T(8,128)(2,1)} copy(bf16[392,6144]{1,0:T(8,128)(2,1)} %convolution_convert_fusion.2) | data formatting | bytes 9633792
  163.4 0.2 reduce-scatter.6.cloned.1.call-start
  163.6 9.9 %fusion = bf16[6144,768]{0,1:T(8,128)(2,1)} fusion(bf16[392,768]{1,0:T(8,128)(2,1)S(1)} %bitcast.26, bf16[392,6144]{1,0:T(8,128)(2,1)} %all-gather.5.cloned.1.call-done), kind=kOutput, calls=%fused_computation.2 | convolution fusion | flops 3704094720 | bytes 14856192 | tf_op jit(solution)/shard_map/dot_general | solution.py:75
  173.6 0.4 multiply_convert_fusion
  174.0 10.3 %convolution_convert_fusion = bf16[768,6144]{1,0:T(8,128)(2,1)} fusion(bf16[392,768]{1,0:T(8,128)(2,1)S(1)} %bitcast.27, bf16[392,6144]{1,0:T(8,128)(2,1)} %all-gather.3.cloned.1.call-done), kind=kOutput, calls=%fused_computation | convolution fusion | flops 3704094720 | bytes 14856192 | tf_op jit(solution)/shard_map/dot_general | solution.py:54
  184.4 0.1 stack.39
  184.5 7.8 %all-reduce.2 = (f32[9,768]{1,0:T(8,128)}, f32[768]{0:T(1024)}) all-reduce(f32[9,768]{1,0:T(8,128)S(1)} %stack.39, f32[768]{0:T(1024)S(1)} %get-tuple-element.24), channel_id=1, replica_groups=mesh['space'=2,'tensor'=16] {'space'}, use_global_device_ids=true, to_apply=%region_12.13 | all-reduce | flops 7680 | bytes 61440 | tf_op jit(solution)/shard_map/psum | solution.py:65
  192.3 53.8 %reduce-scatter.10.cloned.1.call-done = bf16[384,392]{1,0:T(8,128)(2,1)} async-done(((bf16[6144,392]{1,0:T(8,128)(2,1)}), bf16[384,392]{1,0:T(8,128)(2,1)}) %reduce-scatter.10.cloned.1.call-update) | async-done | bytes 301072
  246.1 1.9 copy.14
  247.9 110.1 %reduce-scatter.6.cloned.1.call-done = bf16[3072,768]{0,1:T(8,128)(2,1)} async-done(((bf16[6144,768]{0,1:T(8,128)(2,1)}), bf16[3072,768]{0,1:T(8,128)(2,1)}) %reduce-scatter.6.cloned.1.call-update) | async-done | bytes 4718608 | tf_op jit(solution)/shard_map/reduce_scatter | solution.py:79
  358.0 6.6 %copy.12 = bf16[3072,768]{1,0:T(8,128)(2,1)} copy(bf16[3072,768]{0,1:T(8,128)(2,1)} %reduce-scatter.6.cloned.1.call-done) | data formatting | bytes 9437184
  364.6 106.8 %reduce-scatter.8.cloned.1.call-done = bf16[768,3072]{1,0:T(8,128)(2,1)} async-done(((bf16[768,6144]{1,0:T(8,128)(2,1)}), bf16[768,3072]{1,0:T(8,128)(2,1)}) %reduce-scatter.8.cloned.1.call-update) | async-done | bytes 4718608 | tf_op jit(solution)/shard_map/reduce_scatter | solution.py:82
  (27 shorter events, 0.3 us)
Async XLA Ops:
  7.2 62.3 %all-gather.5.cloned.1.call-start = ((), (), s32[]{:S(2)}) async-start(), calls=%async_computation.4 | async-start | bytes 5117952 | tf_op jit(solution)/shard_map/all_gather | solution.py:38
  7.9 118.6 %all-gather.3.cloned.1.call-start = ((), (), s32[]{:S(2)}) async-start(), calls=%async_computation.3 | async-start | bytes 5117952 | tf_op jit(solution)/shard_map/all_gather | solution.py:39
  8.7 237.4 %reduce-scatter.10.cloned.1.call-start = ((), (), s32[]{:S(2)}) async-start(), calls=%async_computation.7 | async-start | bytes 6684672
  78.6 56.2 %collective-permute-start = (bf16[1,56,768]{2,1,0:T(8,128)(2,1)S(1)}, bf16[1,56,768]{2,1,0:T(8,128)(2,1)S(1)}, u32[]{:S(2)}, u32[]{:S(2)}) collective-permute-start(bf16[1,56,768]{2,1,0:T(8,128)(2,1)S(1)} %get-tuple-element.40), channel_id=1, source_target_pairs={{0,16},{1,17},{2,18},{3,19},{4,20},{5,21},{6,22},{7,23},{8,24},{9,... | collective-permute-start | bytes 258056 | tf_op jit(solution)/shard_map/ppermute | solution.py:15
  82.0 52.8 %collective-permute-start.1 = (bf16[1,56,768]{2,1,0:T(8,128)(2,1)S(1)}, bf16[1,56,768]{2,1,0:T(8,128)(2,1)S(1)}, u32[]{:S(2)}, u32[]{:S(2)}) collective-permute-start(bf16[1,56,768]{2,1,0:T(8,128)(2,1)S(1)} %get-tuple-element.41), channel_id=1, source_target_pairs={{16,0},{17,1},{18,2},{19,3},{20,4},{21,5},{22,6},{23,7},{24,8},{25... | collective-permute-start | bytes 258056 | tf_op jit(solution)/shard_map/ppermute | solution.py:18
  134.8 0.7 copy-start
  135.5 14.0 %slice-start = ((s8[9437184]{0:T(1024)(128)(4,1)}), s8[4194304]{0:T(1024)(128)(4,1)S(1)}, s32[]{:S(2)}) async-start(s8[9437184]{0:T(1024)(128)(4,1)} %bitcast.29), calls=%async_computation.8 | async-start | bytes 8388608
  135.5 14.0 %slice-start.1 = ((s8[9437184]{0:T(1024)(128)(4,1)}), s8[4194304]{0:T(1024)(128)(4,1)S(1)}, s32[]{:S(2)}) async-start(s8[9437184]{0:T(1024)(128)(4,1)} %bitcast.29), calls=%async_computation.9 | async-start | bytes 8388608
  138.6 5.6 %collective-permute-start.2 = (bf16[1,56,768]{2,1,0:T(8,128)(2,1)S(1)}, bf16[1,56,768]{2,1,0:T(8,128)(2,1)S(1)}, u32[]{:S(2)}, u32[]{:S(2)}) collective-permute-start(bf16[1,56,768]{2,1,0:T(8,128)(2,1)S(1)} %get-tuple-element.38), channel_id=1, source_target_pairs={{0,16},{1,17},{2,18},{3,19},{4,20},{5,21},{6,22},{7,23},{8,24},{9,... | collective-permute-start | bytes 258056 | tf_op jit(solution)/shard_map/ppermute | solution.py:15
  142.0 6.4 %collective-permute-start.3 = (bf16[1,56,768]{2,1,0:T(8,128)(2,1)S(1)}, bf16[1,56,768]{2,1,0:T(8,128)(2,1)S(1)}, u32[]{:S(2)}, u32[]{:S(2)}) collective-permute-start(bf16[1,56,768]{2,1,0:T(8,128)(2,1)S(1)} %get-tuple-element.39), channel_id=1, source_target_pairs={{16,0},{17,1},{18,2},{19,3},{20,4},{21,5},{22,6},{23,7},{24,8},{25... | collective-permute-start | bytes 258056 | tf_op jit(solution)/shard_map/ppermute | solution.py:18
  148.6 1.2 slice-start.2
  163.4 194.6 %reduce-scatter.6.cloned.1.call-start = ((), (), s32[]{:S(2)}) async-start(), calls=%async_computation.5 | async-start | bytes 14155776 | tf_op jit(solution)/shard_map/reduce_scatter | solution.py:79
  173.6 297.9 %reduce-scatter.8.cloned.1.call-start = ((), (), s32[]{:S(2)}) async-start(), calls=%async_computation.6 | async-start | bytes 14155776 | tf_op jit(solution)/shard_map/reduce_scatter | solution.py:82
Sparse Core Ops, SparseCore 0:
  10.2 59.3 all-gather.4
  71.7 54.7 all-gather.2
  163.5 82.4 reduce-scatter.9
  248.3 109.6 reduce-scatter.5
  360.9 110.5 reduce-scatter.7
where the time goes:
time: 479 us; the launch traced here: 478 us
  waiting for transfers between devices  380 us (79%)
  matrix products  43 us (9%)
  local copies, waits for them, and re-layouts  18.5 us (4%)
  between operations  14 us (3%)
  starting transfers between devices  9.73 us (2%)
  blocking collectives  7.82 us (2%)
  other arithmetic  4.79 us (1%)
    reduce_scatter x1, waiting for transfers between devices, shards(): lax.psum_scatter(in_term.astype(jnp.bfloat16), 'space', scatter_dimension...  110 us
    reduce_scatter x1, waiting for transfers between devices, shards(): lax.psum_scatter(out_term.astype(jnp.bfloat16), 'space', scatter_dimensio...  107 us
    all_gather x1, waiting for transfers between devices, shards(): lax.all_gather(tokens, 'tensor', axis=1, tiled=True)  59.7 us
    unnamed x6, waiting for transfers between devices  55.2 us
    all_gather x1, waiting for transfers between devices, shards(): lax.all_gather(grad_out, 'tensor', axis=1, tiled=True)  43.2 us
    unnamed x11, local copies, waits for them, and re-layouts  17.2 us
    dot_general x1, matrix products, shards(): lax.dot_general(act, full_grad, (((0,), (0,)), ((), ())), preferred_eleme...  10.3 us
    dot_general x1, matrix products, shards(): lax.dot_general(full_tokens, grad_hidden, (((0,), (0,)), ((), ())), prefe...  9.91 us
  transfers between devices with their start and end apart: 9, of which 7 were waited for; matrix products, arithmetic and copies ran while one was open for 10% of the time, Pallas kernels for 0%

commit v1 on v0

--- a/solution.py
+++ b/solution.py
@@ -5,6 +5,24 @@
 
 GW = 56
 OFFSETS = [(-1, -1), (-1, 0), (-1, 1), (0, -1), (0, 0), (0, 1), (1, -1), (1, 0), (1, 1)]
+
+
+def ring_gather(array, axis, dim):
+    ways, here, lap = (lax.axis_size(axis), lax.axis_index(axis), array.shape[dim])
+    shape = [n * ways if d == dim else n for d, n in enumerate(array.shape)]
+    full = lax.dynamic_update_slice_in_dim(
+        jnp.zeros(shape, array.dtype), array, here * lap, axis=dim
+    )
+    going_up = going_down = array
+    for far in range(1, ways // 2 + 1):
+        going_up = lax.ppermute(going_up, axis, [(d, (d + 1) % ways) for d in range(ways)])
+        full = lax.dynamic_update_slice_in_dim(full, going_up, (here - far) % ways * lap, axis=dim)
+        if 2 * far < ways:
+            going_down = lax.ppermute(going_down, axis, [(d, (d - 1) % ways) for d in range(ways)])
+            full = lax.dynamic_update_slice_in_dim(
+                full, going_down, (here + far) % ways * lap, axis=dim
+            )
+    return full
 
 
 def padded_2(block, sides, width):
@@ -35,7 +53,7 @@
     grid_rows = tok_rows // GW
     ff_local = w_in.shape[1]
     full_tokens, full_grad = (
-        lax.all_gather(tokens, "tensor", axis=1, tiled=True),
+        ring_gather(tokens, "tensor", 1),
         lax.all_gather(grad_out, "tensor", axis=1, tiled=True),
     )
     hidden_acc = jnp.dot(full_tokens, w_in, preferred_element_type=jnp.float32)

time: 479 us -> 460 us (0.960)
  waiting for transfers between devices: 380 us -> 342 us
  starting transfers between devices: 9.73 us -> 40.1 us
  local copies, waits for them, and re-layouts: 18.5 us -> 12 us
    all_gather x1 -> x0, waiting for transfers between devices: 59.7 us -> none  [shards(): lax.all_gather(tokens, 'tensor', axis=1, tiled=True)]
    ppermute x0 -> x15, waiting for transfers between devices: none -> 54.8 us  [the longest x8 54.3 us: ring_gather(): lax.ppermute(going_up, axis, [(d, (d + 1) % ways) for d in range(ways)])]
    all_gather x1, waiting for transfers between devices: 43.2 us -> 0.02 us  [shards(): lax.all_gather(grad_out, 'tensor', axis=1, tiled=True)]
    ppermute x0 -> x15, starting transfers between devices: none -> 32.7 us  [the longest x7 27.9 us: ring_gather(): lax.ppermute(going_down, axis, [(d, (d - 1) % ways) for d in range(ways)])]
    unnamed x11 -> x18, local copies, waits for them, and re-layouts: 17.2 us -> 10.2 us
    dot_general x1, matrix products: 9.03 us -> 4.14 us  [shards(): hidden_acc = jnp.dot(full_tokens, w_in, preferred_element_type=jnp.float32)]
    unnamed x6 -> x5, waiting for transfers between devices: 55.2 us -> 52.8 us
  transfers between devices with their start and end apart: 9 -> 23, of which waited for: 7 -> 16; matrix products, arithmetic and copies ran while one was open for 10% -> 6% of each run, Pallas kernels for 0% -> 0%
where the time goes in v1:
time: 460 us; the launch traced here: 459 us
  waiting for transfers between devices  342 us (74%)
  starting transfers between devices  40.1 us (9%)
  matrix products  38.6 us (8%)
  between operations  14.2 us (3%)
  local copies, waits for them, and re-layouts  12 us (3%)
  blocking collectives  7.82 us (2%)
  other arithmetic  4.82 us (1%)
    reduce_scatter x1, waiting for transfers between devices, shards(): lax.psum_scatter(in_term.astype(jnp.bfloat16), 'space', scatter_dimension...  113 us
    reduce_scatter x1, waiting for transfers between devices, shards(): lax.psum_scatter(out_term.astype(jnp.bfloat16), 'space', scatter_dimensio...  111 us
    ppermute x8, waiting for transfers between devices, ring_gather(): lax.ppermute(going_up, axis, [(d, (d + 1) % ways) for d in range(ways)])  54.3 us
    unnamed x5, waiting for transfers between devices  52.8 us
    ppermute x7, starting transfers between devices, ring_gather(): lax.ppermute(going_down, axis, [(d, (d - 1) % ways) for d in range(ways)])  27.9 us
    dot_general x1, matrix products, shards(): lax.dot_general(full_tokens, grad_hidden, (((0,), (0,)), ((), ())), prefe...  10.4 us
    unnamed x18, local copies, waits for them, and re-layouts  10.2 us
    dot_general x1, matrix products, shards(): lax.dot_general(act, full_grad, (((0,), (0,)), ((), ())), preferred_eleme...  10.2 us
  transfers between devices with their start and end apart: 23, of which 16 were waited for; matrix products, arithmetic and copies ran while one was open for 6% of the time, Pallas kernels for 0%

profile of v1, /device:TPU:0, one launch (start us, length us, event | category | flops | bytes accessed | tf_op | source)
XLA Modules:
  0.0 459.5 jit_solution(612479269263891161)
XLA Ops:
  8.4 5.0 %collective-permute-start.1 = (bf16[392,384]{1,0:T(8,128)(2,1)}, bf16[392,384]{1,0:T(8,128)(2,1)S(1)}, u32[]{:S(2)}, u32[]{:S(2)}) collective-permute-start(bf16[392,384]{1,0:T(8,128)(2,1)} %param.6), channel_id=1, source_target_pairs={{0,15},{1,0},{2,1},{3,2},{4,3},{5,4},{6,5},{7,6},{8,7},{9,8},{10,9... | collective-permute-start | bytes 903176 | tf_op jit(solution)/shard_map/ppermute | solution.py:21
  13.5 4.7 %collective-permute-done = bf16[392,384]{1,0:T(8,128)(2,1)S(1)} collective-permute-done((bf16[392,384]{1,0:T(8,128)(2,1)}, bf16[392,384]{1,0:T(8,128)(2,1)S(1)}, u32[]{:S(2)}, u32[]{:S(2)}) %collective-permute-start) | collective-permute-done | bytes 301088 | tf_op jit(solution)/shard_map/ppermute | solution.py:18
  18.4 4.3 collective-permute-start.3
  22.7 5.7 %collective-permute-done.2 = bf16[392,384]{1,0:T(8,128)(2,1)S(1)} collective-permute-done((bf16[392,384]{1,0:T(8,128)(2,1)S(1)}, bf16[392,384]{1,0:T(8,128)(2,1)S(1)}, u32[]{:S(2)}, u32[]{:S(2)}) %collective-permute-start.2) | collective-permute-done | bytes 301088 | tf_op jit(solution)/shard_map/ppermute | solution.py:18
  28.4 2.5 collective-permute-start.4
  30.9 1.9 collective-permute-start.5
  32.8 6.4 %collective-permute-done.4 = bf16[392,384]{1,0:T(8,128)(2,1)S(1)} collective-permute-done((bf16[392,384]{1,0:T(8,128)(2,1)S(1)}, bf16[392,384]{1,0:T(8,128)(2,1)S(1)}, u32[]{:S(2)}, u32[]{:S(2)}) %collective-permute-start.4) | collective-permute-done | bytes 301088 | tf_op jit(solution)/shard_map/ppermute | solution.py:18
  40.0 4.5 collective-permute-start.7
  44.5 3.7 collective-permute-done.6
  48.8 4.7 %collective-permute-start.9 = (bf16[392,384]{1,0:T(8,128)(2,1)S(1)}, bf16[392,384]{1,0:T(8,128)(2,1)S(1)}, u32[]{:S(2)}, u32[]{:S(2)}) collective-permute-start(bf16[392,384]{1,0:T(8,128)(2,1)S(1)} %collective-permute-done.7), channel_id=1, source_target_pairs={{0,15},{1,0},{2,1},{3,2},{4,3},{5,4},{6,5},{7,6},{8,7},{9,8},{10,9... | collective-permute-start | bytes 903176 | tf_op jit(solution)/shard_map/ppermute | solution.py:21
  53.6 9.0 %collective-permute-done.8 = bf16[392,384]{1,0:T(8,128)(2,1)S(1)} collective-permute-done((bf16[392,384]{1,0:T(8,128)(2,1)S(1)}, bf16[392,384]{1,0:T(8,128)(2,1)S(1)}, u32[]{:S(2)}, u32[]{:S(2)}) %collective-permute-start.8) | collective-permute-done | bytes 301088 | tf_op jit(solution)/shard_map/ppermute | solution.py:18
  62.7 4.5 collective-permute-start.11
  67.3 6.2 %collective-permute-done.10 = bf16[392,384]{1,0:T(8,128)(2,1)S(1)} collective-permute-done((bf16[392,384]{1,0:T(8,128)(2,1)S(1)}, bf16[392,384]{1,0:T(8,128)(2,1)S(1)}, u32[]{:S(2)}, u32[]{:S(2)}) %collective-permute-start.10) | collective-permute-done | bytes 301088 | tf_op jit(solution)/shard_map/ppermute | solution.py:18
  73.4 1.6 collective-permute-start.12
  75.2 2.9 collective-permute-start.13
  78.1 10.1 %collective-permute-done.12 = bf16[392,384]{1,0:T(8,128)(2,1)S(1)} collective-permute-done((bf16[392,384]{1,0:T(8,128)(2,1)S(1)}, bf16[392,384]{1,0:T(8,128)(2,1)S(1)}, u32[]{:S(2)}, u32[]{:S(2)}) %collective-permute-start.12) | collective-permute-done | bytes 301088 | tf_op jit(solution)/shard_map/ppermute | solution.py:18
  88.5 8.7 %collective-permute-done.14 = bf16[392,384]{1,0:T(8,128)(2,1)S(1)} collective-permute-done((bf16[392,384]{1,0:T(8,128)(2,1)S(1)}, bf16[392,384]{1,0:T(8,128)(2,1)S(1)}, u32[]{:S(2)}, u32[]{:S(2)}) %collective-permute-start.14) | collective-permute-done | bytes 301088 | tf_op jit(solution)/shard_map/ppermute | solution.py:18
  97.2 4.1 convolution_convert_fusion.3
  101.4 3.0 collective-permute-start.15
  106.5 4.3 collective-permute-done.16
  111.0 8.3 %fusion.35 = f32[392,768]{1,0:T(8,128)S(1)} fusion(bf16[392,6144]{1,0:T(8,128)(2,1)} %all-gather.2.cloned.1.call-done, bf16[768,6144]{1,0:T(8,128)(2,1)} %param.9), kind=kOutput, calls=%fused_computation.92 | convolution fusion | flops 3699376128 | bytes 15458304 | tf_op jit(solution)/shard_map/dot_general | solution.py:60
  119.3 3.1 fusion.16
  126.1 4.3 collective-permute-done.18
  131.9 5.6 %convolution_convert_fusion.2 = bf16[392,6144]{1,0:T(8,128)(2,1)} fusion(bf16[392,768]{1,0:T(8,128)(2,1)S(1)} %bitcast.23, bf16[6144,768]{1,0:T(8,128)(2,1)S(1)} %bitcast.28), kind=kOutput, calls=%fused_computation.2 | convolution fusion | flops 3701784576 | bytes 14856192 | tf_op jit(solution)/shard_map/dot_general | solution.py:106
  137.5 8.0 %copy.11 = bf16[392,6144]{0,1:T(8,128)(2,1)} copy(bf16[392,6144]{1,0:T(8,128)(2,1)} %convolution_convert_fusion.2) | data formatting | bytes 9633792
  145.9 10.2 %convolution_convert_fusion.1 = bf16[768,6144]{1,0:T(8,128)(2,1)} fusion(bf16[392,768]{1,0:T(8,128)(2,1)S(1)} %bitcast.25, bf16[392,6144]{1,0:T(8,128)(2,1)} %all-gather.2.cloned.1.call-done), kind=kOutput, calls=%fused_computation.1 | convolution fusion | flops 3704094720 | bytes 14856192 | tf_op jit(solution)/shard_map/dot_general | solution.py:72
  156.2 10.4 %convolution_convert_fusion = bf16[6144,768]{1,0:T(8,128)(2,1)} fusion(bf16[392,6144]{1,0:T(8,128)(2,1)} %copy-done, bf16[392,768]{1,0:T(8,128)(2,1)S(1)} %bitcast.24), kind=kOutput, calls=%fused_computation | convolution fusion | flops 3704094720 | bytes 14856192 | tf_op jit(solution)/shard_map/dot_general | solution.py:93
  166.8 7.8 %all-reduce.2 = (f32[9,768]{1,0:T(8,128)}, f32[768]{0:T(1024)}) all-reduce(f32[9,768]{1,0:T(8,128)S(1)} %stack.39, f32[768]{0:T(1024)S(1)} %get-tuple-element.14), channel_id=1, replica_groups=mesh['space'=2,'tensor'=16] {'space'}, use_global_device_ids=true, to_apply=%region_12.13 | all-reduce | flops 7680 | bytes 61440 | tf_op jit(solution)/shard_map/psum | solution.py:83
  174.6 52.1 %reduce-scatter.10.cloned.1.call-done = bf16[384,392]{1,0:T(8,128)(2,1)} async-done(((bf16[6144,392]{1,0:T(8,128)(2,1)}), bf16[384,392]{1,0:T(8,128)(2,1)}) %reduce-scatter.10.cloned.1.call-update) | async-done | bytes 301072
  226.7 1.9 copy.12
  228.6 110.9 %reduce-scatter.8.cloned.1.call-done = bf16[768,3072]{1,0:T(8,128)(2,1)} async-done(((bf16[768,6144]{1,0:T(8,128)(2,1)}), bf16[768,3072]{1,0:T(8,128)(2,1)}) %reduce-scatter.8.cloned.1.call-update) | async-done | bytes 4718608 | tf_op jit(solution)/shard_map/reduce_scatter | solution.py:100
  339.5 113.4 %reduce-scatter.6.cloned.1.call-done = bf16[3072,768]{1,0:T(8,128)(2,1)} async-done(((bf16[6144,768]{1,0:T(8,128)(2,1)}), bf16[3072,768]{1,0:T(8,128)(2,1)}) %reduce-scatter.6.cloned.1.call-update) | async-done | bytes 4718608 | tf_op jit(solution)/shard_map/reduce_scatter | solution.py:97
  (78 shorter events, 11.5 us)
Async XLA Ops:
  7.2 103.9 %all-gather.2.cloned.1.call-start = ((), (), s32[]{:S(2)}) async-start(), calls=%async_computation.3 | async-start | bytes 5117952 | tf_op jit(solution)/shard_map/all_gather | solution.py:57
  7.9 218.8 %reduce-scatter.10.cloned.1.call-start = ((), (), s32[]{:S(2)}) async-start(), calls=%async_computation.6 | async-start | bytes 6684672
  7.9 10.3 %collective-permute-start = (bf16[392,384]{1,0:T(8,128)(2,1)}, bf16[392,384]{1,0:T(8,128)(2,1)S(1)}, u32[]{:S(2)}, u32[]{:S(2)}) collective-permute-start(bf16[392,384]{1,0:T(8,128)(2,1)} %param.6), channel_id=1, source_target_pairs={{0,1},{1,2},{2,3},{3,4},{4,5},{5,6},{6,7},{7,8},{8,9},{9,10},{10,1... | collective-permute-start | bytes 903176 | tf_op jit(solution)/shard_map/ppermute | solution.py:18
  8.4 9.9 %collective-permute-start.1 = (bf16[392,384]{1,0:T(8,128)(2,1)}, bf16[392,384]{1,0:T(8,128)(2,1)S(1)}, u32[]{:S(2)}, u32[]{:S(2)}) collective-permute-start(bf16[392,384]{1,0:T(8,128)(2,1)} %param.6), channel_id=1, source_target_pairs={{0,15},{1,0},{2,1},{3,2},{4,3},{5,4},{6,5},{7,6},{8,7},{9,8},{10,9... | collective-permute-start | bytes 903176 | tf_op jit(solution)/shard_map/ppermute | solution.py:21
  18.2 10.2 %collective-permute-start.2 = (bf16[392,384]{1,0:T(8,128)(2,1)S(1)}, bf16[392,384]{1,0:T(8,128)(2,1)S(1)}, u32[]{:S(2)}, u32[]{:S(2)}) collective-permute-start(bf16[392,384]{1,0:T(8,128)(2,1)S(1)} %collective-permute-done), channel_id=1, source_target_pairs={{0,1},{1,2},{2,3},{3,4},{4,5},{5,6},{6,7},{7,8},{8,9},{9,10},{10,1... | collective-permute-start | bytes 903176 | tf_op jit(solution)/shard_map/ppermute | solution.py:18
  18.4 12.5 %collective-permute-start.3 = (bf16[392,384]{1,0:T(8,128)(2,1)S(1)}, bf16[392,384]{1,0:T(8,128)(2,1)S(1)}, u32[]{:S(2)}, u32[]{:S(2)}) collective-permute-start(bf16[392,384]{1,0:T(8,128)(2,1)S(1)} %collective-permute-done.1), channel_id=1, source_target_pairs={{0,15},{1,0},{2,1},{3,2},{4,3},{5,4},{6,5},{7,6},{8,7},{9,8},{10,9... | collective-permute-start | bytes 903176 | tf_op jit(solution)/shard_map/ppermute | solution.py:21
  28.4 10.8 %collective-permute-start.4 = (bf16[392,384]{1,0:T(8,128)(2,1)S(1)}, bf16[392,384]{1,0:T(8,128)(2,1)S(1)}, u32[]{:S(2)}, u32[]{:S(2)}) collective-permute-start(bf16[392,384]{1,0:T(8,128)(2,1)S(1)} %collective-permute-done.2), channel_id=1, source_target_pairs={{0,1},{1,2},{2,3},{3,4},{4,5},{5,6},{6,7},{7,8},{8,9},{9,10},{10,1... | collective-permute-start | bytes 903176 | tf_op jit(solution)/shard_map/ppermute | solution.py:18
  30.9 9.1 %collective-permute-start.5 = (bf16[392,384]{1,0:T(8,128)(2,1)S(1)}, bf16[392,384]{1,0:T(8,128)(2,1)S(1)}, u32[]{:S(2)}, u32[]{:S(2)}) collective-permute-start(bf16[392,384]{1,0:T(8,128)(2,1)S(1)} %collective-permute-done.3), channel_id=1, source_target_pairs={{0,15},{1,0},{2,1},{3,2},{4,3},{5,4},{6,5},{7,6},{8,7},{9,8},{10,9... | collective-permute-start | bytes 903176 | tf_op jit(solution)/shard_map/ppermute | solution.py:21
  32.8 7.0 %copy-start.1 = (bf16[392,384]{1,0:T(8,128)(2,1)S(1)}, bf16[392,384]{1,0:T(8,128)(2,1)}, u32[]{:S(2)}) copy-start(bf16[392,384]{1,0:T(8,128)(2,1)} %param.6) | copy-start | bytes 903172
  39.2 9.0 %collective-permute-start.6 = (bf16[392,384]{1,0:T(8,128)(2,1)S(1)}, bf16[392,384]{1,0:T(8,128)(2,1)S(1)}, u32[]{:S(2)}, u32[]{:S(2)}) collective-permute-start(bf16[392,384]{1,0:T(8,128)(2,1)S(1)} %collective-permute-done.4), channel_id=1, source_target_pairs={{0,1},{1,2},{2,3},{3,4},{4,5},{5,6},{6,7},{7,8},{8,9},{9,10},{10,1... | collective-permute-start | bytes 903176 | tf_op jit(solution)/shard_map/ppermute | solution.py:18
  39.8 57.4 %copy-start.4 = (bf16[6144,768]{1,0:T(8,128)(2,1)S(1)}, bf16[6144,768]{1,0:T(8,128)(2,1)}, u32[]{:S(2)}) copy-start(bf16[6144,768]{1,0:T(8,128)(2,1)} %param.8) | copy-start | bytes 28311556
  40.0 8.8 %collective-permute-start.7 = (bf16[392,384]{1,0:T(8,128)(2,1)S(1)}, bf16[392,384]{1,0:T(8,128)(2,1)S(1)}, u32[]{:S(2)}, u32[]{:S(2)}) collective-permute-start(bf16[392,384]{1,0:T(8,128)(2,1)S(1)} %collective-permute-done.5), channel_id=1, source_target_pairs={{0,15},{1,0},{2,1},{3,2},{4,3},{5,4},{6,5},{7,6},{8,7},{9,8},{10,9... | collective-permute-start | bytes 903176 | tf_op jit(solution)/shard_map/ppermute | solution.py:21
  48.2 14.3 %collective-permute-start.8 = (bf16[392,384]{1,0:T(8,128)(2,1)S(1)}, bf16[392,384]{1,0:T(8,128)(2,1)S(1)}, u32[]{:S(2)}, u32[]{:S(2)}) collective-permute-start(bf16[392,384]{1,0:T(8,128)(2,1)S(1)} %collective-permute-done.6), channel_id=1, source_target_pairs={{0,1},{1,2},{2,3},{3,4},{4,5},{5,6},{6,7},{7,8},{8,9},{9,10},{10,1... | collective-permute-start | bytes 903176 | tf_op jit(solution)/shard_map/ppermute | solution.py:18
  48.8 13.9 %collective-permute-start.9 = (bf16[392,384]{1,0:T(8,128)(2,1)S(1)}, bf16[392,384]{1,0:T(8,128)(2,1)S(1)}, u32[]{:S(2)}, u32[]{:S(2)}) collective-permute-start(bf16[392,384]{1,0:T(8,128)(2,1)S(1)} %collective-permute-done.7), channel_id=1, source_target_pairs={{0,15},{1,0},{2,1},{3,2},{4,3},{5,4},{6,5},{7,6},{8,7},{9,8},{10,9... | collective-permute-start | bytes 903176 | tf_op jit(solution)/shard_map/ppermute | solution.py:21
  62.5 10.9 %collective-permute-start.10 = (bf16[392,384]{1,0:T(8,128)(2,1)S(1)}, bf16[392,384]{1,0:T(8,128)(2,1)S(1)}, u32[]{:S(2)}, u32[]{:S(2)}) collective-permute-start(bf16[392,384]{1,0:T(8,128)(2,1)S(1)} %collective-permute-done.8), channel_id=1, source_target_pairs={{0,1},{1,2},{2,3},{3,4},{4,5},{5,6},{6,7},{7,8},{8,9},{9,10},{10,1... | collective-permute-start | bytes 903176 | tf_op jit(solution)/shard_map/ppermute | solution.py:18
  62.7 12.5 %collective-permute-start.11 = (bf16[392,384]{1,0:T(8,128)(2,1)S(1)}, bf16[392,384]{1,0:T(8,128)(2,1)S(1)}, u32[]{:S(2)}, u32[]{:S(2)}) collective-permute-start(bf16[392,384]{1,0:T(8,128)(2,1)S(1)} %collective-permute-done.9), channel_id=1, source_target_pairs={{0,15},{1,0},{2,1},{3,2},{4,3},{5,4},{6,5},{7,6},{8,7},{9,8},{10,9... | collective-permute-start | bytes 903176 | tf_op jit(solution)/shard_map/ppermute | solution.py:21
  73.4 14.8 %collective-permute-start.12 = (bf16[392,384]{1,0:T(8,128)(2,1)S(1)}, bf16[392,384]{1,0:T(8,128)(2,1)S(1)}, u32[]{:S(2)}, u32[]{:S(2)}) collective-permute-start(bf16[392,384]{1,0:T(8,128)(2,1)S(1)} %collective-permute-done.10), channel_id=1, source_target_pairs={{0,1},{1,2},{2,3},{3,4},{4,5},{5,6},{6,7},{7,8},{8,9},{9,10},{10,1... | collective-permute-start | bytes 903176 | tf_op jit(solution)/shard_map/ppermute | solution.py:18
  75.2 13.2 %collective-permute-start.13 = (bf16[392,384]{1,0:T(8,128)(2,1)S(1)}, bf16[392,384]{1,0:T(8,128)(2,1)S(1)}, u32[]{:S(2)}, u32[]{:S(2)}) collective-permute-start(bf16[392,384]{1,0:T(8,128)(2,1)S(1)} %collective-permute-done.11), channel_id=1, source_target_pairs={{0,15},{1,0},{2,1},{3,2},{4,3},{5,4},{6,5},{7,6},{8,7},{9,8},{10,9... | collective-permute-start | bytes 903176 | tf_op jit(solution)/shard_map/ppermute | solution.py:21
  88.2 8.9 %collective-permute-start.14 = (bf16[392,384]{1,0:T(8,128)(2,1)S(1)}, bf16[392,384]{1,0:T(8,128)(2,1)S(1)}, u32[]{:S(2)}, u32[]{:S(2)}) collective-permute-start(bf16[392,384]{1,0:T(8,128)(2,1)S(1)} %collective-permute-done.12), channel_id=1, source_target_pairs={{0,1},{1,2},{2,3},{3,4},{4,5},{5,6},{6,7},{7,8},{8,9},{9,10},{10,1... | collective-permute-start | bytes 903176 | tf_op jit(solution)/shard_map/ppermute | solution.py:18
  97.2 4.2 copy-start
  97.2 8.5 %copy-start.2 = (f32[9,768]{1,0:T(8,128)S(1)}, f32[9,768]{1,0:T(8,128)}, u32[]{:S(2)}) copy-start(f32[9,768]{1,0:T(8,128)} %param.10) | copy-start | bytes 82948
  101.4 5.1 %collective-permute-start.15 = (bf16[1,56,768]{2,1,0:T(8,128)(2,1)S(1)}, bf16[1,56,768]{2,1,0:T(8,128)(2,1)S(1)}, u32[]{:S(2)}, u32[]{:S(2)}) collective-permute-start(bf16[1,56,768]{2,1,0:T(8,128)(2,1)S(1)} %get-tuple-element.30), channel_id=1, source_target_pairs={{0,16},{1,17},{2,18},{3,19},{4,20},{5,21},{6,22},{7,23},{8,24},{9,... | collective-permute-start | bytes 258056 | tf_op jit(solution)/shard_map/ppermute | solution.py:33
  104.4 6.4 %collective-permute-start.16 = (bf16[1,56,768]{2,1,0:T(8,128)(2,1)S(1)}, bf16[1,56,768]{2,1,0:T(8,128)(2,1)S(1)}, u32[]{:S(2)}, u32[]{:S(2)}) collective-permute-start(bf16[1,56,768]{2,1,0:T(8,128)(2,1)S(1)} %get-tuple-element.31), channel_id=1, source_target_pairs={{16,0},{17,1},{18,2},{19,3},{20,4},{21,5},{22,6},{23,7},{24,8},{25... | collective-permute-start | bytes 258056 | tf_op jit(solution)/shard_map/ppermute | solution.py:36
  111.0 8.3 %copy-start.3 = (f32[768]{0:T(1024)S(1)}, f32[768]{0:T(1024)}, u32[]{:S(2)}) copy-start(f32[768]{0:T(1024)} %param.11) | copy-start | bytes 9220
  119.3 12.2 %slice-start = ((s8[9437184]{0:T(1024)(128)(4,1)}), s8[4194304]{0:T(1024)(128)(4,1)S(1)}, s32[]{:S(2)}) async-start(s8[9437184]{0:T(1024)(128)(4,1)} %bitcast.27), calls=%async_computation.7 | async-start | bytes 8388608
  119.3 12.2 %slice-start.1 = ((s8[9437184]{0:T(1024)(128)(4,1)}), s8[4194304]{0:T(1024)(128)(4,1)S(1)}, s32[]{:S(2)}) async-start(s8[9437184]{0:T(1024)(128)(4,1)} %bitcast.27), calls=%async_computation.8 | async-start | bytes 8388608
  122.5 3.6 collective-permute-start.17
  124.0 6.4 %collective-permute-start.18 = (bf16[1,56,768]{2,1,0:T(8,128)(2,1)S(1)}, bf16[1,56,768]{2,1,0:T(8,128)(2,1)S(1)}, u32[]{:S(2)}, u32[]{:S(2)}) collective-permute-start(bf16[1,56,768]{2,1,0:T(8,128)(2,1)S(1)} %get-tuple-element.29), channel_id=1, source_target_pairs={{16,0},{17,1},{18,2},{19,3},{20,4},{21,5},{22,6},{23,7},{24,8},{25... | collective-permute-start | bytes 258056 | tf_op jit(solution)/shard_map/ppermute | solution.py:36
  130.6 1.2 slice-start.2
  145.5 194.1 %reduce-scatter.8.cloned.1.call-start = ((), (), s32[]{:S(2)}) async-start(), calls=%async_computation.5 | async-start | bytes 14155776 | tf_op jit(solution)/shard_map/reduce_scatter | solution.py:100
  156.1 296.8 %reduce-scatter.6.cloned.1.call-start = ((), (), s32[]{:S(2)}) async-start(), calls=%async_computation.4 | async-start | bytes 14155776 | tf_op jit(solution)/shard_map/reduce_scatter | solution.py:97
Sparse Core Ops, SparseCore 0:
  10.2 77.3 all-gather.1
  145.6 81.0 reduce-scatter.9
  229.7 109.7 reduce-scatter.7
  342.4 110.5 reduce-scatter.5
